TPU v7x, 128 devices: a whole 4x4x4 slice. The times are simulated.
128 devices in a mesh: row: 16 (over x, z), col: 8 (over y, core).
Axes of the slice: x: 4, y: 4, z: 4, core: 2. Of those that a mesh axis runs over, the one named last changes fastest.
Arguments:
- blocks: bfloat16 [512, 16, 128, 128], P('row', 'col'), may hold values from -0.375 to 0.375
- pattern: int32 [512, 16], replicated, may hold values from 0 to 511, as said below
- owners: int32 [8, 512, 2, 1], P('col', 'row'), may hold values from 0 to 15; in each aligned block of 64 rows (0 to 63, 64 to 127, ..., all dimensions but the last counted through in order) at most 6 rows name the same one
Outputs:
- moved: bfloat16 [8, 16, 96, 128, 128], P('col', 'row')
Inputs may be any that keep to these rules, and one draw needn't show every extreme that they name: `pattern`: block row i holds 16 distinct column blocks (i + d) mod 512, by rising d with |d| <= 8, d = 0 among them, in slot order. `owners`: among the 64 entries of one device no value occurs more than 6 times; in some device some value occurs exactly 6 times.
All inputs are finite; a program needn't handle non-finite values.
Results may differ from a plain program's by a relative error of at most 0.0049.
Values may be sent and summed in bfloat16 or wider, within the bound.
No kernel may reach another device: no remote copies, remote signals or barrier semaphores. Data moves between devices by JAX's collectives and lax.ppermute only.
A program may use at most 192 MiB of HBM per device.

v0:
```python
import math

import jax
import jax.numpy as jnp
from jax import lax
from jax.sharding import PartitionSpec as P


def extended_2(shard, sides, width):
    for axis, dim in sides:
        devices, length = (lax.axis_size(axis), shard.shape[dim])
        up = [(i, (i + 1) % devices) for i in range(devices)]
        down = [(j, i) for i, j in up]
        last = lax.slice_in_dim(shard, length - width, length, axis=dim)
        first = lax.slice_in_dim(shard, 0, width, axis=dim)
        before = lax.ppermute(last, axis, up)
        after = lax.ppermute(first, axis, down)
        shard = jnp.concatenate([before, shard, after], axis=dim)
    return shard


def local_index(pattern, start_row, row_count, margin, slot_start, target_count):
    nblk, slot_count = pattern.shape
    reach = slot_count // 2
    own_cols = lax.dynamic_slice_in_dim(pattern, start_row, row_count, 0)
    row_ids = start_row + jnp.arange(row_count, dtype=jnp.int32)
    offsets = (own_cols - row_ids[:, None] + reach + nblk) % nblk - reach
    ext_row = jnp.arange(row_count, dtype=jnp.int32)[:, None] + margin + offsets
    neighbour_cols = pattern[own_cols]
    wanted = lax.dynamic_slice_in_dim(own_cols, slot_start, target_count, 1)
    same_col = neighbour_cols[:, None, :, :] == wanted[:, :, None, None]
    has_match = jnp.any(same_col, axis=-1)
    match_slot = jnp.sum(
        same_col.astype(jnp.int32) * jnp.arange(slot_count, dtype=jnp.int32), axis=-1
    )
    extent = (row_count + 2 * margin) * slot_count
    return jnp.where(has_match, ext_row[:, None, :] * slot_count + match_slot, extent)


def multiply(left, extended, pick_index):
    row_count, slot_count, tile_size = (left.shape[0], left.shape[1], left.shape[-1])
    target_count = pick_index.shape[1]
    group_rows = math.gcd(row_count, max(1, 32 // target_count))
    flat_table = jnp.concatenate(
        [
            extended.reshape(-1, tile_size, tile_size),
            jnp.zeros((1, tile_size, tile_size), extended.dtype),
        ],
        axis=0,
    )

    def per_group(operands):
        left_rows, pick_rows = operands
        picked = flat_table[pick_rows]
        return jnp.einsum("gtab,gstbc->gsac", left_rows, picked, preferred_element_type=jnp.float32)

    result = lax.map(
        per_group,
        (
            left.reshape(row_count // group_rows, group_rows, slot_count, tile_size, tile_size),
            pick_index.reshape(row_count // group_rows, group_rows, target_count, slot_count),
        ),
    )
    return result.reshape(row_count, target_count, tile_size, tile_size)


def per_device(blocks, pattern, owners):
    row_count, slot_share, tile_size = (blocks.shape[0], blocks.shape[1], blocks.shape[-1])
    slot_count = pattern.shape[1]
    reach = slot_count // 2
    row_pos = lax.axis_index("row")
    col_pos = lax.axis_index("col")
    row_devices = lax.axis_size("row")
    full_rows = lax.all_gather(blocks, "col", axis=1, tiled=True)
    extended = extended_2(full_rows, (("row", 0),), reach)
    pick_index = local_index(
        pattern, row_pos * row_count, row_count, reach, col_pos * slot_share, slot_share
    )
    squared = multiply(full_rows, extended, pick_index).astype(jnp.bfloat16)
    square_rows = lax.all_gather(squared, "col", axis=1, tiled=True)
    cube_term = multiply(square_rows, extended, pick_index)
    result = (3.0 * squared.astype(jnp.float32) - 2.0 * cube_term).astype(jnp.bfloat16)
    block_count = row_count * slot_share
    capacity = 3 * block_count // (2 * row_devices)
    flat_result = result.reshape(block_count, tile_size, tile_size)
    destination = owners.reshape(block_count)
    one_hot = (destination[:, None] == jnp.arange(row_devices, dtype=jnp.int32)[None, :]).astype(
        jnp.int32
    )
    bucket_rank = jnp.sum((jnp.cumsum(one_hot, axis=0) - 1) * one_hot, axis=1)
    bucket_slot = destination * capacity + bucket_rank
    wanted = jnp.arange(row_devices * capacity, dtype=jnp.int32)
    slot_match = bucket_slot[None, :] == wanted[:, None]
    has_source = jnp.any(slot_match, axis=1)
    source = jnp.sum(
        slot_match.astype(jnp.int32) * jnp.arange(block_count, dtype=jnp.int32)[None, :], axis=1
    )
    padded = jnp.concatenate(
        [flat_result, jnp.zeros((1, tile_size, tile_size), flat_result.dtype)], axis=0
    )
    buckets = padded[jnp.where(has_source, source, block_count)].reshape(
        row_devices, capacity, tile_size, tile_size
    )
    received = lax.all_to_all(buckets, "row", split_axis=0, concat_axis=0, tiled=True)
    return received.reshape(1, 1, row_devices * capacity, tile_size, tile_size)


def solution(mesh):
    in_specs = (P("row", "col", None, None), P(), P("col", "row", None, None))
    out_specs = P("col", "row", None, None, None)
    return jax.shard_map(
        per_device, mesh=mesh, in_specs=in_specs, out_specs=out_specs, check_vma=False
    )
```

profile of v0, /device:TPU:8, one launch (start us, length us, event | category | flops | bytes accessed | tf_op | source)
XLA Modules:
  0.0 546.1 jit_solution(1662284565458652383)
XLA Ops:
  6.5 0.7 all-gather.3.cloned.1.call-update
  7.3 88.5 %all-gather.3.cloned.1.call-done = bf16[32,16,128,128]{3,2,1,0:T(8,128)(2,1)} async-done(((bf16[32,2,128,128]{3,2,1,0:T(8,128)(2,1)}), bf16[32,16,128,128]{3,2,1,0:T(8,128)(2,1)}) %all-gather.3.cloned.1.call-update) | async-done | bytes 16777232 | tf_op jit(solution)/shard_map/all_gather | solution.py:74
  95.9 6.0 %fusion.20 = (bf16[8,16,128,128]{3,2,1,0:T(8,128)(2,1)}, bf16[8,16,128,128]{3,2,1,0:T(8,128)(2,1)}) fusion(bf16[32,16,128,128]{3,2,1,0:T(8,128)(2,1)} %all-gather.3.cloned.1.call-done), kind=kLoop, calls=%fused_computation.45 | loop fusion | bytes 16777216 | tf_op jit(solution)/shard_map/slice | solution.py:14
  101.9 1.6 collective-permute-start
  103.4 3.8 collective-permute-start.1
  107.2 0.1 copy.35
  107.6 1.0 gather_fusion.2
  108.7 0.2 copy.36
  109.4 0.5 broadcast_convert_fusion
  109.9 88.4 %collective-permute-done = bf16[8,16,128,128]{3,2,1,0:T(8,128)(2,1)} collective-permute-done((bf16[8,16,128,128]{3,2,1,0:T(8,128)(2,1)}, bf16[8,16,128,128]{3,2,1,0:T(8,128)(2,1)}, u32[]{:S(2)}, u32[]{:S(2)}) %collective-permute-start) | collective-permute-done | bytes 4194336 | tf_op jit(solution)/shard_map/ppermute | solution.py:16
  198.3 17.7 %pad_maximum_fusion = bf16[48,16,128,128]{3,2,1,0:T(8,128)(2,1)} fusion(bf16[8,16,128,128]{3,2,1,0:T(8,128)(2,1)} %collective-permute-done.1, bf16[32,16,128,128]{3,2,1,0:T(8,128)(2,1)} %all-gather.3.cloned.1.call-done, bf16[8,16,128,128]{3,2,1,0:T(8,128)(2,1)} %collective-permute-done), kind=kLoop, calls=%fused_computation.18 | loop fusion | flops 25165824 | bytes 50331648 | tf_op jit(solution)/shard_map/concatenate | solution.py:18
  216.0 22.0 %concatenate.11 = bf16[769,128,128]{2,1,0:T(8,128)(2,1)} pad(bf16[768,128,128]{2,1,0:T(8,128)(2,1)} %bitcast.93, bf16[]{:T(256)} %constant.99.clone.1), padding=0_1x0_0x0_0 | pad | bytes 50364416 | tf_op jit(solution)/shard_map/concatenate | solution.py:44
  237.9 66.4 %while.22 = (s32[]{:T(128)}, bf16[2,16,2,128,128]{3,4,2,1,0:T(8,128)(2,1)S(1)}, s32[2,16,2,16]{3,2,1,0:T(2,128)S(1)}, bf16[769,128,128]{2,1,0:T(8,128)(2,1)}, bf16[2,16,16,128,128]{4,3,2,1,0:T(8,128)(2,1)}) while((s32[]{:T(128)}, bf16[2,16,2,128,128]{3,4,2,1,0:T(8,128)(2,1)S(1)}, s32[2,16,2,16]{3,2,1,0:T(2,128)S(1)}, ...), condition=%wide.region_3.4_spmd.clone, body=%wide.region_2.3_spmd.sunk.clone | while | flops 2147486208 | bytes 60834880 | solution.py:57
  238.1 21.9 %gather_fusion = bf16[512,128,128]{2,1,0:T(8,128)(2,1)} fusion(bf16[769,128,128]{2,1,0:T(8,128)(2,1)} %get-tuple-element.196, s32[1024]{0:T(1024)S(1)} %pad_clamp_fusion.8), kind=kCustom, calls=%fused_computation.clone.1.clone | custom fusion | bytes 33556480 | tf_op jit(solution)/shard_map/while/body/eval_jaxpr/gather | solution.py:54
  259.9 11.2 %bitcast_dynamic-update-slice_fusion.6 = bf16[2,16,2,128,128]{3,4,2,1,0:T(8,128)(2,1)S(1)} fusion(bf16[2,16,2,128,128]{3,4,2,1,0:T(8,128)(2,1)S(1)} %get-tuple-element.189, s32[]{:T(128)} %get-tuple-element.188, bf16[16,2,16,128,128]{4,3,2,1,0:T(8,128)(2,1)} %bitcast.91, bf16[2,16,16,128,128]{4,3,2,1,0:T(8,128)(2,1)} %get-tuple-element.197), kind=kOutput, calls=%fused_computation.7.clone.1.clone | convolution fusion | flops 2147483648 | bytes 27264000 | tf_op jit(solution)/shard_map/while/body/eval_jaxpr/gtab,gstbc->gsac/dot_general | solution.py:55
  271.2 21.9 %gather_fusion = bf16[512,128,128]{2,1,0:T(8,128)(2,1)} fusion(bf16[769,128,128]{2,1,0:T(8,128)(2,1)} %get-tuple-element.196, s32[1024]{0:T(1024)S(1)} %pad_clamp_fusion.8), kind=kCustom, calls=%fused_computation.clone.1.clone | custom fusion | bytes 33556480 | tf_op jit(solution)/shard_map/while/body/eval_jaxpr/gather | solution.py:54
  293.1 11.2 %bitcast_dynamic-update-slice_fusion.6 = bf16[2,16,2,128,128]{3,4,2,1,0:T(8,128)(2,1)S(1)} fusion(bf16[2,16,2,128,128]{3,4,2,1,0:T(8,128)(2,1)S(1)} %get-tuple-element.189, s32[]{:T(128)} %get-tuple-element.188, bf16[16,2,16,128,128]{4,3,2,1,0:T(8,128)(2,1)} %bitcast.91, bf16[2,16,16,128,128]{4,3,2,1,0:T(8,128)(2,1)} %get-tuple-element.197), kind=kOutput, calls=%fused_computation.7.clone.1.clone | convolution fusion | flops 2147483648 | bytes 27264000 | tf_op jit(solution)/shard_map/while/body/eval_jaxpr/gtab,gstbc->gsac/dot_general | solution.py:55
  304.3 1.3 copy-done
  306.0 0.2 select_reduce_fusion.1
  306.5 84.6 %all-gather.5.cloned.1.call-done = bf16[32,16,128,128]{2,3,1,0:T(8,128)(2,1)} async-done(((bf16[32,2,128,128]{2,3,1,0:T(8,128)(2,1)}), bf16[32,16,128,128]{2,3,1,0:T(8,128)(2,1)}) %all-gather.5.cloned.1.call-update) | async-done | bytes 16777232 | tf_op jit(solution)/shard_map/all_gather | solution.py:80
  391.1 22.5 %copy.41 = bf16[32,16,128,128]{3,2,1,0:T(8,128)(2,1)} copy(bf16[32,16,128,128]{2,3,1,0:T(8,128)(2,1)} %all-gather.5.cloned.1.call-done) | data formatting | bytes 33554432 | tf_op jit(solution)/shard_map/all_gather | solution.py:80
  413.6 67.6 %while.23 = (s32[]{:T(128)}, f32[2,16,2,128,128]{3,4,2,1,0:T(8,128)}, s32[2,16,2,16]{3,2,1,0:T(2,128)S(1)}, bf16[769,128,128]{2,1,0:T(8,128)(2,1)}, bf16[2,16,16,128,128]{4,3,2,1,0:T(8,128)(2,1)}) while((s32[]{:T(128)}, f32[2,16,2,128,128]{3,4,2,1,0:T(8,128)}, s32[2,16,2,16]{3,2,1,0:T(2,128)S(1)}, ...), condition=%wide.region_5.6_spmd.clone, body=%wide.region_4.5_spmd.sunk.clone | while | flops 2147486208 | bytes 60834880 | solution.py:57
  413.7 22.0 %gather_fusion.1 = bf16[512,128,128]{2,1,0:T(8,128)(2,1)} fusion(bf16[769,128,128]{2,1,0:T(8,128)(2,1)} %get-tuple-element.211, s32[1024]{0:T(1024)S(1)} %pad_clamp_fusion.9), kind=kCustom, calls=%fused_computation.1.clone.1.clone | custom fusion | bytes 33556480 | tf_op jit(solution)/shard_map/while/body/eval_jaxpr/gather | solution.py:54
  435.7 11.7 %bitcast_dynamic-update-slice_fusion.7 = f32[2,16,2,128,128]{3,4,2,1,0:T(8,128)} fusion(f32[2,16,2,128,128]{3,4,2,1,0:T(8,128)} %get-tuple-element.204, s32[]{:T(128)} %get-tuple-element.203, bf16[16,2,16,128,128]{4,3,2,1,0:T(8,128)(2,1)} %bitcast.92, bf16[2,16,16,128,128]{4,3,2,1,0:T(8,128)(2,1)} %get-tuple-element.212), kind=kOutput, calls=%fused_computation.14.clone.1.clone | convolution fusion | flops 2147483648 | bytes 27264000 | tf_op jit(solution)/shard_map/while/body/eval_jaxpr/gtab,gstbc->gsac/dot_general | solution.py:55
  447.6 21.9 %gather_fusion.1 = bf16[512,128,128]{2,1,0:T(8,128)(2,1)} fusion(bf16[769,128,128]{2,1,0:T(8,128)(2,1)} %get-tuple-element.211, s32[1024]{0:T(1024)S(1)} %pad_clamp_fusion.9), kind=kCustom, calls=%fused_computation.1.clone.1.clone | custom fusion | bytes 33556480 | tf_op jit(solution)/shard_map/while/body/eval_jaxpr/gather | solution.py:54
  469.4 11.8 %bitcast_dynamic-update-slice_fusion.7 = f32[2,16,2,128,128]{3,4,2,1,0:T(8,128)} fusion(f32[2,16,2,128,128]{3,4,2,1,0:T(8,128)} %get-tuple-element.204, s32[]{:T(128)} %get-tuple-element.203, bf16[16,2,16,128,128]{4,3,2,1,0:T(8,128)(2,1)} %bitcast.92, bf16[2,16,16,128,128]{4,3,2,1,0:T(8,128)(2,1)} %get-tuple-element.212), kind=kOutput, calls=%fused_computation.14.clone.1.clone | convolution fusion | flops 2147483648 | bytes 27264000 | tf_op jit(solution)/shard_map/while/body/eval_jaxpr/gtab,gstbc->gsac/dot_general | solution.py:55
  481.2 2.9 subtract_convert_fusion
  484.2 0.2 concatenate.12
  484.3 2.7 gather_fusion.3
  487.0 3.5 copy.44
  490.5 47.0 %all_to_all.5 = bf16[16,6,128,128]{3,2,1,0:T(8,128)(2,1)S(1)} all-to-all(bf16[16,6,128,128]{3,2,1,0:T(8,128)(2,1)S(1)} %bitcast.97), channel_id=1, replica_groups=mesh['row'=16,'col'=8] {'row'}, dimensions={0} | all-to-all | bytes 6291456 | tf_op jit(solution)/shard_map/all_to_all | solution.py:104
  537.6 1.7 copy.69
  (46 shorter events, 1.9 us)
Async XLA Ops:
  6.5 89.3 %all-gather.3.cloned.1.call-start = ((), (), s32[]{:S(2)}) async-start(), calls=%async_computation.1 | async-start | bytes 18874368 | tf_op jit(solution)/shard_map/all_gather | solution.py:74
  7.3 100.0 %copy-start.2 = (s32[512,16]{0,1:T(8,128)S(1)}, s32[512,16]{0,1:T(8,128)}, u32[]{:S(2)}) copy-start(s32[512,16]{0,1:T(8,128)} %param.8) | copy-start | bytes 98308
  7.3 383.8 %all-gather.5.cloned.1.call-start = ((), (), s32[]{:S(2)}) async-start(), calls=%async_computation.2 | async-start | bytes 18874368 | tf_op jit(solution)/shard_map/all_gather | solution.py:80
  101.9 96.4 %collective-permute-start = (bf16[8,16,128,128]{3,2,1,0:T(8,128)(2,1)}, bf16[8,16,128,128]{3,2,1,0:T(8,128)(2,1)}, u32[]{:S(2)}, u32[]{:S(2)}) collective-permute-start(bf16[8,16,128,128]{3,2,1,0:T(8,128)(2,1)} %get-tuple-element.91), channel_id=1, source_target_pairs={{0,8},{8,16},{16,24},{24,32},{32,40},{40,48},{48,56},{56,64},{64,7... | collective-permute-start | bytes 12582920 | tf_op jit(solution)/shard_map/ppermute | solution.py:16
  103.4 94.8 %collective-permute-start.1 = (bf16[8,16,128,128]{3,2,1,0:T(8,128)(2,1)}, bf16[8,16,128,128]{3,2,1,0:T(8,128)(2,1)}, u32[]{:S(2)}, u32[]{:S(2)}) collective-permute-start(bf16[8,16,128,128]{3,2,1,0:T(8,128)(2,1)} %get-tuple-element.92), channel_id=1, source_target_pairs={{8,0},{16,8},{24,16},{32,24},{40,32},{48,40},{56,48},{64,56},{72,6... | collective-permute-start | bytes 12582920 | tf_op jit(solution)/shard_map/ppermute | solution.py:17
  237.9 67.7 %copy-start.3 = (s32[1,32,2,1]{1,3,2,0:T(1,128)S(1)}, s32[1,32,2,1]{1,3,2,0:T(1,128)}, u32[]{:S(2)}) copy-start(s32[1,32,2,1]{1,3,2,0:T(1,128)} %param.9) | copy-start | bytes 772
  304.3 1.3 copy-start
  413.6 67.6 %copy-start.1 = (bf16[2,16,2,128,128]{3,4,2,1,0:T(8,128)(2,1)S(1)}, bf16[2,16,2,128,128]{3,4,2,1,0:T(8,128)(2,1)}, u32[]{:S(2)}) copy-start(bf16[2,16,2,128,128]{3,4,2,1,0:T(8,128)(2,1)} %copy-done) | copy-start | bytes 6291460
Sparse Core Ops, SparseCore 0:
  9.0 86.7 all-gather.2
  305.8 85.2 all-gather.4
where the time goes:
time: 547 us; the launch traced here: 546 us
  waiting for transfers between devices  262 us (48%)
  local copies, waits for them, and re-layouts  150 us (27%)
  blocking collectives  47 us (9%)
  matrix products  45.9 us (8%)
  other arithmetic  22 us (4%)
  between operations  13.6 us (2%)
    all_gather x1, waiting for transfers between devices, per_device(): full_rows = lax.all_gather(blocks, 'col', axis=1, tiled=True)  88.5 us
    ppermute x1, waiting for transfers between devices, extended_2(): before = lax.ppermute(last, axis, up)  88.4 us
    gather x4, local copies, waits for them, and re-layouts, per_group(): picked = flat_table[pick_rows]  87.6 us
    all_gather x1, waiting for transfers between devices, per_device(): square_rows = lax.all_gather(squared, 'col', axis=1, tiled=True)  84.6 us
    all_to_all x1, blocking collectives, per_device(): lax.all_to_all(buckets, 'row', split_axis=0, concat_axis=0, tiled=True)  47 us
    dot_general x4, matrix products, per_group(): jnp.einsum('gtab,gstbc->gsac', left_rows, picked, preferred_element_type=...  45.9 us
    all_gather x1, local copies, waits for them, and re-layouts, per_device(): square_rows = lax.all_gather(squared, 'col', axis=1, tiled=True)  22.5 us
    concatenate x1, local copies, waits for them, and re-layouts, multiply(): jnp.concatenate([extended.reshape(-1, tile_size, tile_size), jnp.zeros((1...  22 us
  transfers between devices with their start and end apart: 4, of which 3 were waited for; matrix products, arithmetic and copies ran while one was open for 1% of the time, Pallas kernels for 0%

commit v1 on v0

v1 whole, which is shorter than its diff:
```python
import jax
import jax.numpy as jnp
from jax import lax
from jax.experimental import pallas as pl
from jax.experimental.pallas import tpu as pltpu
from jax.sharding import PartitionSpec as P

T = 128
REACH = 8
OWN = 4
SPAN = OWN + 2 * REACH
SLOTS = 16
NEAR = OWN * SLOTS
FAR = 43
CUT = NEAR - FAR


def tile_sl(k):
    return pl.ds(k * T, T)


def purify_kernel(cols, missing, core, own, before, after, far, relayed, out, band, squared, result, in_sem, out_sem):
    def fetch(ref, shift, row, slot):
        flat = (slot // 2) * (2 * OWN) + (row % OWN) * 2 + slot % 2 - shift
        dst = band.at[tile_sl(row), pl.ds(pl.multiple_of((cols[row * SLOTS + slot] + 1) * T, T), T)]
        pltpu.make_async_copy(ref.at[flat], dst, in_sem).start()

    def fetch_far(low, high):
        for row in range(4):
            for slot in range(7 - row, SLOTS):
                fetch(low, CUT, row, slot)
        for row in range(16, 20):
            for slot in range(0, 28 - row):
                fetch(high, 0, row, slot)

    for row in range(8, 12):
        for slot in range(SLOTS):
            fetch(own, 0, row, slot)
    for row in range(4, 8):
        for slot in range(7 - row, SLOTS):
            if slot >= 0:
                fetch(before, 0, row, slot)
    for row in range(12, 16):
        for slot in range(0, min(SLOTS, 28 - row)):
            fetch(after, 0, row, slot)

    @pl.when(core[0] == 0)
    def _():
        fetch_far(far, relayed)

    @pl.when(core[0] != 0)
    def _():
        fetch_far(relayed, far)

    zero = jnp.zeros((T, T), jnp.bfloat16)
    for row in range(SPAN):
        for col in range(SPAN):
            inside = abs(row // 2 - col // 2) <= 4 or 8 <= row < 12
            if abs(row - col) > REACH and inside:
                band[tile_sl(row), tile_sl(col + 1)] = zero
        spot = pl.multiple_of((missing[row] + 1) * T, T)
        band[tile_sl(row), pl.ds(spot, T)] = zero

    all_in = band.at[pl.ds(0, 264 * 8), pl.ds(0, 2048)]
    pltpu.make_async_copy(all_in, all_in, in_sem).wait()

    half = SPAN // 2
    for j in range(half):
        k0, k1 = max(0, j - 4) * 2 * T, min(half, j + 5) * 2 * T
        acc = jnp.dot(
            band[8 * T : 12 * T, T + k0 : T + k1],
            band[k0:k1, T + j * 2 * T : T + (j + 1) * 2 * T],
            preferred_element_type=jnp.float32,
        )
        squared[:, j * 2 * T : (j + 1) * 2 * T] = acc.astype(jnp.bfloat16)
    for a in range(OWN):
        for col in range(SPAN):
            if abs(col - a - REACH) > REACH:
                squared[tile_sl(a), tile_sl(col)] = zero
        squared[tile_sl(a), pl.ds(pl.multiple_of(missing[REACH + a] * T, T), T)] = zero
    for j in range(half):
        k0, k1 = max(0, j - 4) * 2 * T, min(half, j + 5) * 2 * T
        cube = jnp.dot(
            squared[:, k0:k1],
            band[k0:k1, T + j * 2 * T : T + (j + 1) * 2 * T],
            preferred_element_type=jnp.float32,
        )
        cut = slice(j * 2 * T, (j + 1) * 2 * T)
        result[:, cut] = (3.0 * squared[:, cut].astype(jnp.float32) - 2.0 * cube).astype(jnp.bfloat16)
    for a in range(OWN):
        for slot in range(SLOTS):
            flat = (slot // 2) * (2 * OWN) + a * 2 + slot % 2
            src = result.at[tile_sl(a), pl.ds(pl.multiple_of(cols[(REACH + a) * SLOTS + slot] * T, T), T)]
            pltpu.make_async_copy(src, out.at[flat], out_sem).start()
    all_out = result.at[:, pl.ds(0, 2048)]
    pltpu.make_async_copy(all_out, all_out, out_sem).wait()


def purify(cols, missing, core, own, before, after, far, relayed):
    smem = pl.BlockSpec(memory_space=pltpu.SMEM)
    hbm = pl.BlockSpec(memory_space=pl.ANY)
    return pl.pallas_call(
        purify_kernel,
        out_shape=jax.ShapeDtypeStruct((NEAR, T, T), jnp.bfloat16),
        in_specs=[smem] * 3 + [hbm] * 5,
        out_specs=hbm,
        scratch_shapes=[
            pltpu.VMEM((SPAN * T, (SPAN + 2) * T), jnp.bfloat16),
            pltpu.VMEM((OWN * T, SPAN * T), jnp.bfloat16),
            pltpu.VMEM((OWN * T, SPAN * T), jnp.bfloat16),
            pltpu.SemaphoreType.DMA,
            pltpu.SemaphoreType.DMA,
        ],
        compiler_params=pltpu.CompilerParams(vmem_limit_bytes=60 << 20),
        cost_estimate=pl.CostEstimate(flops=9_400_000_000, bytes_accessed=11_000_000, transcendentals=0),
        name="purify",
    )(cols, missing, core, own, before, after, far, relayed)


def bucket_kernel(source, blocks, out, held, in_sem, out_sem):
    count = out.shape[0]
    load = pltpu.make_async_copy(blocks, held.at[pl.ds(0, NEAR)], in_sem)
    load.start()
    held[NEAR] = jnp.zeros((T, T), jnp.bfloat16)
    load.wait()
    for k in range(count):
        pltpu.make_async_copy(held.at[source[k]], out.at[k], out_sem).start()
    pltpu.make_async_copy(out, out, out_sem).wait()


def bucket(source, blocks):
    count = source.shape[0]
    return pl.pallas_call(
        bucket_kernel,
        out_shape=jax.ShapeDtypeStruct((count, T, T), jnp.bfloat16),
        in_specs=[pl.BlockSpec(memory_space=pltpu.SMEM), pl.BlockSpec(memory_space=pl.ANY)],
        out_specs=pl.BlockSpec(memory_space=pl.ANY),
        scratch_shapes=[
            pltpu.VMEM((NEAR + 1, T, T), jnp.bfloat16),
            pltpu.SemaphoreType.DMA,
            pltpu.SemaphoreType.DMA,
        ],
        compiler_params=pltpu.CompilerParams(vmem_limit_bytes=60 << 20),
        cost_estimate=pl.CostEstimate(flops=0, bytes_accessed=7_000_000, transcendentals=0),
        name="bucket",
    )(source, blocks)


def bucket_source(owners, devices):
    count = owners.size
    capacity = 3 * count // (2 * devices)
    destination = owners.reshape(count)
    index = jnp.arange(count, dtype=jnp.int32)
    same = (destination[:, None] == destination[None, :]) & (index[None, :] < index[:, None])
    rank = jnp.sum(same.astype(jnp.int32), axis=1)
    place = destination * capacity + rank
    wanted = jnp.arange(devices * capacity, dtype=jnp.int32)
    match = place[None, :] == wanted[:, None]
    return count + jnp.sum(jnp.where(match, index[None, :] - count, 0), axis=1)


def per_device(blocks, pattern, owners):
    both = ("row", "col")
    nblk = pattern.shape[0]
    cols_n = lax.axis_size("col")
    rows_n = lax.axis_size("row")
    total = rows_n * cols_n
    c = lax.axis_index("col")
    me = lax.axis_index("row") * cols_n + c
    core = c % 2

    rows = me * OWN - REACH + jnp.arange(SPAN, dtype=jnp.int32)
    wrapped = (rows + nblk) % nblk
    offset = (pattern[wrapped] - wrapped[:, None] + REACH + nblk) % nblk - REACH
    place = jnp.arange(SPAN, dtype=jnp.int32)
    cols = (place[:, None] + offset).reshape(-1)
    missing = jnp.clip(place - jnp.sum(offset, axis=1), -1, SPAN)

    own = lax.all_to_all(blocks.reshape(cols_n, 2 * OWN, T, T), "col", split_axis=0, concat_axis=0, tiled=True)
    own = own.reshape(NEAR, T, T)
    before = lax.ppermute(own, both, [(i, (i + 1) % total) for i in range(total)])
    after = lax.ppermute(own, both, [((i + 1) % total, i) for i in range(total)])
    far_out = lax.dynamic_slice_in_dim(own, CUT * (1 - core), FAR, 0)
    far = lax.ppermute(far_out, both, [(i, (i + 2 - 4 * (i % 2)) % total) for i in range(total)])
    relay_out = jnp.where(core == 0, before[CUT:], after[:FAR])
    relayed = lax.ppermute(relay_out, both, [(i, i ^ 1) for i in range(total)])

    result = purify(cols, missing, core.reshape(1), own, before, after, far, relayed)
    mine = lax.all_to_all(result.reshape(cols_n, 2 * OWN, T, T), "col", split_axis=0, concat_axis=0, tiled=True)
    buckets = bucket(bucket_source(owners, rows_n), mine.reshape(NEAR, T, T))
    buckets = buckets.reshape(rows_n, -1, T, T)
    received = lax.all_to_all(buckets, "row", split_axis=0, concat_axis=0, tiled=True)
    return received.reshape(1, 1, -1, T, T)


def solution(mesh):
    in_specs = (P("row", "col", None, None), P(), P("col", "row", None, None))
    out_specs = P("col", "row", None, None, None)
    return jax.shard_map(per_device, mesh=mesh, in_specs=in_specs, out_specs=out_specs, check_vma=False)
```

time: 547 us -> 184 us (0.34)
  waiting for transfers between devices: 262 us -> 64.5 us
  local copies, waits for them, and re-layouts: 150 us -> 4.2 us
  matrix products: 45.9 us -> 0 us
  blocking collectives: 47 us -> 77.3 us
  Pallas kernels: 0 us -> 19.2 us
  other arithmetic: 22 us -> 5.3 us
  between operations: 13.6 us -> 0.11 us
  starting transfers between devices: 5.39 us -> 11.5 us
    all_gather x2 -> x0, waiting for transfers between devices: 173 us -> none  [the longest x1 88.5 us: per_device(): full_rows = lax.all_gather(blocks, 'col', axis=1, tiled=True)]
    gather x8 -> x1, local copies, waits for them, and re-layouts: 95 us -> 0.56 us  [per_device(): offset = (pattern[wrapped] - wrapped[:, None] + REACH + nblk) % nblk - REACH]
    ppermute x2 -> x4, waiting for transfers between devices: 88.4 us -> 39.8 us  [the longest x1 38.7 us: per_device(): lax.ppermute(own, both, [(i, (i + 1) % total) for i in range(total)])]
    dot_general x4 -> x0, matrix products: 45.9 us -> none  [per_group(): jnp.einsum('gtab,gstbc->gsac', left_rows, picked, preferred_element_type=...]
    all_to_all x0 -> x1, blocking collectives: none -> 30.9 us  [per_device(): lax.all_to_all(blocks.reshape(cols_n, 2 * OWN, T, T), 'col', split_axis=0...]
    all_to_all x0 -> x1, waiting for transfers between devices: none -> 24.7 us  [per_device(): lax.all_to_all(result.reshape(cols_n, 2 * OWN, T, T), 'col', split_axis=0...]
    all_gather x1 -> x0, local copies, waits for them, and re-layouts: 22.5 us -> none  [per_device(): square_rows = lax.all_gather(squared, 'col', axis=1, tiled=True)]
    concatenate x2 -> x0, local copies, waits for them, and re-layouts: 22.2 us -> none  [the longest x1 22 us: multiply(): jnp.concatenate([extended.reshape(-1, tile_size, tile_size), jnp.zeros((1...]
  transfers between devices with their start and end apart: 4 -> 5, of which waited for: 3 -> 3; matrix products, arithmetic and copies ran while one was open for 1% -> 4% of each run, Pallas kernels for 0% -> 0%
where the time goes in v1:
time: 184 us; the launch traced here: 182 us
  blocking collectives  77.3 us (42%)
  waiting for transfers between devices  64.5 us (35%)
  Pallas kernels  19.2 us (10%)
  starting transfers between devices  11.5 us (6%)
  other arithmetic  5.3 us (3%)
  local copies, waits for them, and re-layouts  4.2 us (2%)
    all_to_all x1, blocking collectives, per_device(): lax.all_to_all(buckets, 'row', split_axis=0, concat_axis=0, tiled=True)  46.4 us
    ppermute x1, waiting for transfers between devices, per_device(): lax.ppermute(own, both, [(i, (i + 1) % total) for i in range(total)])  38.7 us
    all_to_all x1, blocking collectives, per_device(): lax.all_to_all(blocks.reshape(cols_n, 2 * OWN, T, T), 'col', split_axis=0...  30.9 us
    all_to_all x1, waiting for transfers between devices, per_device(): lax.all_to_all(result.reshape(cols_n, 2 * OWN, T, T), 'col', split_axis=0...  24.7 us
    pallas_call x1, Pallas kernels, purify(): pl.pallas_call(purify_kernel, out_shape=jax.ShapeDtypeStruct((NEAR, T, T)...  15.3 us
    all_to_all x1, starting transfers between devices, per_device(): lax.all_to_all(result.reshape(cols_n, 2 * OWN, T, T), 'col', split_axis=0...  9.58 us
    pallas_call x1, Pallas kernels, bucket(): pl.pallas_call(bucket_kernel, out_shape=jax.ShapeDtypeStruct((count, T, T...  3.88 us
  transfers between devices with their start and end apart: 5, of which 3 were waited for; matrix products, arithmetic and copies ran while one was open for 4% of the time, Pallas kernels for 0%

profile of v1, /device:TPU:8, one launch (start us, length us, event | category | flops | bytes accessed | tf_op | source)
XLA Modules:
  0.0 182.1 jit_solution(2014223854963619574)
XLA Ops:
  0.0 30.9 %all_to_all.15 = bf16[8,8,128,128]{3,2,1,0:T(8,128)(2,1)S(1)} all-to-all(bf16[8,8,128,128]{3,2,1,0:T(8,128)(2,1)} %bitcast.20), channel_id=1, replica_groups=mesh['row'=16,'col'=8] {'col'}, dimensions={0} | all-to-all | bytes 4194304 | tf_op jit(solution)/shard_map/all_to_all | solution.py:179
  30.9 0.0 collective-permute-start
  30.9 1.7 collective-permute-start.1
  32.6 0.1 constant_dynamic-slice_fusion
  32.8 0.0 copy-start.2
  32.8 0.1 collective-permute-start.2
  32.9 38.7 %collective-permute-done.before = bf16[64,128,128]{2,1,0:T(8,128)(2,1)} collective-permute-done((bf16[64,128,128]{2,1,0:T(8,128)(2,1)S(1)}, bf16[64,128,128]{2,1,0:T(8,128)(2,1)}, u32[]{:S(2)}, u32[]{:S(2)}) %collective-permute-start) | collective-permute-done | bytes 2097184 | tf_op jit(solution)/shard_map/ppermute | solution.py:181
  71.6 0.0 collective-permute-done.1.after
  71.6 3.0 %slice_select_fusion = bf16[43,128,128]{2,1,0:T(8,128)(2,1)} fusion(bf16[64,128,128]{2,1,0:T(8,128)(2,1)} %collective-permute-done.1.after, bf16[64,128,128]{2,1,0:T(8,128)(2,1)} %collective-permute-done.before, pred[]{:T(512)S(6)} %eq.41), kind=kLoop, calls=%fused_computation.1 | loop fusion | flops 704512 | bytes 4227073 | tf_op jit(solution)/shard_map/jit(_where)/select_n | solution.py:185
  74.6 0.1 collective-permute-start.3
  74.7 0.1 copy.9
  74.9 0.6 gather_fusion
  75.5 0.2 fusion.3
  75.7 0.1 add.145
  75.7 0.1 add.132
  75.8 0.6 subtract_clamp_fusion.missing
  76.4 0.6 fusion.6.cols
  77.0 0.0 collective-permute-done.2.far
  77.0 1.1 collective-permute-done.3.relayed
  78.1 15.3 %purify.1 = bf16[64,128,128]{2,1,0:T(8,128)(2,1)} custom-call(s32[320]{0:T(512)} %fusion.6.cols, s32[20]{0:T(128)} %subtract_clamp_fusion.missing, s32[1]{0:T(128)} %bitcast.1.core, bf16[64,128,128]{2,1,0:T(8,128)(2,1)} %bitcast.19, bf16[64,128,128]{2,1,0:T(8,128)(2,1)} %collective-permute-done.before, bf16[64,128,128]{2,1,0:T(8,128)(2,1)} %collective-permute-done.1.after, ...), custom_call_target="tpu_custom_call" | custom-call | flops 9400000512 | bytes 11000000 | tf_op jit(solution)/shard_map/purify/pallas_call | solution.py:102
  93.5 0.0 copy-start.3
  93.5 9.6 %all-to-all-start.1 = ((bf16[8,8,128,128]{3,2,1,0:T(8,128)(2,1)}), bf16[8,8,128,128]{3,2,1,0:T(8,128)(2,1)S(1)}, u32[]{:S(2)}, u32[]{:S(2)}) async-start(bf16[8,8,128,128]{3,2,1,0:T(8,128)(2,1)} %bitcast.21), calls=%async_computation.1 | async-start | bytes 4194304 | tf_op jit(solution)/shard_map/all_to_all | solution.py:189
  103.1 0.1 copy.8
  103.2 0.1 reshape.100
  103.3 0.2 convert_reduce_fusion
  103.5 0.1 select_reduce_fusion
  103.6 0.6 broadcast_add_fusion.source
  104.1 24.7 %all-to-all-done.1 = bf16[8,8,128,128]{3,2,1,0:T(8,128)(2,1)S(1)} async-done(((bf16[8,8,128,128]{3,2,1,0:T(8,128)(2,1)}), bf16[8,8,128,128]{3,2,1,0:T(8,128)(2,1)S(1)}, u32[]{:S(2)}, u32[]{:S(2)}) %all-to-all-start.1) | async-done | bytes 2097184 | tf_op jit(solution)/shard_map/all_to_all | solution.py:189
  128.8 1.3 copy-done
  130.1 3.9 %bucket.1 = bf16[96,128,128]{2,1,0:T(8,128)(2,1)} custom-call(s32[96]{0:T(128)} %broadcast_add_fusion.source, bf16[64,128,128]{2,1,0:T(8,128)(2,1)} %bitcast.15), custom_call_target="tpu_custom_call" | custom-call | bytes 7000000 | tf_op jit(solution)/shard_map/bucket/pallas_call | solution.py:133
  134.0 46.4 %all_to_all.16 = bf16[16,6,128,128]{3,2,1,0:T(8,128)(2,1)S(1)} all-to-all(bf16[16,6,128,128]{3,2,1,0:T(8,128)(2,1)} %bitcast.14), channel_id=1, replica_groups=mesh['row'=16,'col'=8] {'row'}, dimensions={0} | all-to-all | bytes 6291456 | tf_op jit(solution)/shard_map/all_to_all | solution.py:192
  180.5 1.7 copy.11
  (10 shorter events, 0.1 us)
Async XLA Ops:
  30.9 43.7 %copy-start.1 = (bf16[8,8,128,128]{3,2,1,0:T(8,128)(2,1)}, bf16[8,8,128,128]{3,2,1,0:T(8,128)(2,1)S(1)}, u32[]{:S(2)}) copy-start(bf16[8,8,128,128]{3,2,1,0:T(8,128)(2,1)S(1)} %all_to_all.15) | copy-start | bytes 6291460
  30.9 40.7 %collective-permute-start = (bf16[64,128,128]{2,1,0:T(8,128)(2,1)S(1)}, bf16[64,128,128]{2,1,0:T(8,128)(2,1)}, u32[]{:S(2)}, u32[]{:S(2)}) collective-permute-start(bf16[64,128,128]{2,1,0:T(8,128)(2,1)S(1)} %bitcast.16), channel_id=1, source_target_pairs={{0,1},{1,2},{2,3},{3,4},{4,5},{5,6},{6,7},{7,8},{8,9},{9,10},{10,1... | collective-permute-start | bytes 6291464 | tf_op jit(solution)/shard_map/ppermute | solution.py:181
  30.9 40.7 %collective-permute-start.1 = (bf16[64,128,128]{2,1,0:T(8,128)(2,1)S(1)}, bf16[64,128,128]{2,1,0:T(8,128)(2,1)}, u32[]{:S(2)}, u32[]{:S(2)}) collective-permute-start(bf16[64,128,128]{2,1,0:T(8,128)(2,1)S(1)} %bitcast.17), channel_id=1, source_target_pairs={{1,0},{2,1},{3,2},{4,3},{5,4},{6,5},{7,6},{8,7},{9,8},{10,9},{11,1... | collective-permute-start | bytes 6291464 | tf_op jit(solution)/shard_map/ppermute | solution.py:182
  32.8 41.9 %copy-start.2 = (s32[512,16]{0,1:T(8,128)S(1)}, s32[512,16]{0,1:T(8,128)}, u32[]{:S(2)}) copy-start(s32[512,16]{0,1:T(8,128)} %param.4) | copy-start | bytes 98308
  32.8 44.2 %collective-permute-start.2 = (bf16[43,128,128]{2,1,0:T(8,128)(2,1)S(1)}, bf16[43,128,128]{2,1,0:T(8,128)(2,1)}, u32[]{:S(2)}, u32[]{:S(2)}) collective-permute-start(bf16[43,128,128]{2,1,0:T(8,128)(2,1)S(1)} %constant_dynamic-slice_fusion), channel_id=1, source_target_pairs={{0,2},{1,127},{2,4},{3,1},{4,6},{5,3},{6,8},{7,5},{8,10},{9,7},{10... | collective-permute-start | bytes 4227080 | tf_op jit(solution)/shard_map/ppermute | solution.py:184
  74.6 3.5 %collective-permute-start.3 = (bf16[43,128,128]{2,1,0:T(8,128)(2,1)}, bf16[43,128,128]{2,1,0:T(8,128)(2,1)}, u32[]{:S(2)}, u32[]{:S(2)}) collective-permute-start(bf16[43,128,128]{2,1,0:T(8,128)(2,1)} %slice_select_fusion), channel_id=1, source_target_pairs={{0,1},{1,0},{2,3},{3,2},{4,5},{5,4},{6,7},{7,6},{8,9},{9,8},{10,11... | collective-permute-start | bytes 4227080 | tf_op jit(solution)/shard_map/ppermute | solution.py:186
  93.5 9.6 %copy-start.3 = (s32[1,32,2,1]{1,3,2,0:T(1,128)S(1)}, s32[1,32,2,1]{1,3,2,0:T(1,128)}, u32[]{:S(2)}) copy-start(s32[1,32,2,1]{1,3,2,0:T(1,128)} %param.5) | copy-start | bytes 772
  93.5 35.3 %all-to-all-start.1 = ((bf16[8,8,128,128]{3,2,1,0:T(8,128)(2,1)}), bf16[8,8,128,128]{3,2,1,0:T(8,128)(2,1)S(1)}, u32[]{:S(2)}, u32[]{:S(2)}) async-start(bf16[8,8,128,128]{3,2,1,0:T(8,128)(2,1)} %bitcast.21), calls=%async_computation.1 | async-start | bytes 4194304 | tf_op jit(solution)/shard_map/all_to_all | solution.py:189
  128.8 1.3 copy-start
